TPU v7x, 32 devices: a whole 2x2x4 slice. The times are simulated.
32 devices in a mesh: parts: 2 (over y), src: 4 (over z), tile: 2 (over x), row: 2 (over core).
Axes of the slice: x: 2, y: 2, z: 4, core: 2. Of those that a mesh axis runs over, the one named last changes fastest.
Arguments:
- mask_windows: float32 [4, 256, 256], P(('parts', 'tile'), ('src', 'row')), parts along dimension 0, may hold values from -4 to 4
- target_windows: float32 [4, 256, 256], P(('parts', 'tile'), ('src', 'row')), parts along dimension 0, may hold values from 0 to 1
- pupil_bands: int32 [24, 128, 2], P(('parts', 'src')), parts along dimension 0, may hold values from 0 to 128, as said below
- pupil_phase: float32 [24, 128, 128], P(('parts', 'src')), parts along dimension 0, may hold values from -3.140625 to 3.140625
- source_weight: float32 [24], P(('parts', 'src')), parts along dimension 0, may hold values from 0.2 to 1
Outputs:
- mask_grad: float32 [4, 256, 256], P(('parts', 'tile'), ('src', 'row')), parts along dimension 0
- source_grad: float32 [24], P(('parts', 'src')), parts along dimension 0
There are 2 independent parts, one for each index of `parts`. A program takes and returns all parts, laid end to end along the dimension named above; each array names one. Nothing has to cross between parts.
Inputs may be any that keep to these rules, and one draw needn't show every extreme that they name: For every source point and frequency row, pupil_bands[s, kx, 0] <= pupil_bands[s, kx, 1]; a row that passes nothing holds (0, 0).
All inputs are finite; a program needn't handle non-finite values.
Results may differ from a plain program's by a relative error of at most 0.00019.
Values sent between devices are 32-bit elements; how exact they have to be, the bound alone decides.
A program may use at most 64 MiB of HBM per device.

v0:
```python
import math
import jax
import jax.numpy as jnp
from jax import lax
from jax.sharding import PartitionSpec as P

M = 256
K = 128
OV = 32
STEEPNESS = 20.0
THRESHOLD = 0.15
LOSS_SCALE = 32.0


def with_halo(block, sides, width):
    for axis, dim in sides:
        count = lax.axis_size(axis)
        forward = [(i, i + 1) for i in range(count - 1)]
        backward = [(target, source) for source, target in forward]
        low = lax.ppermute(
            lax.slice_in_dim(block, block.shape[dim] - width, None, axis=dim), axis, forward
        )
        high = lax.ppermute(lax.slice_in_dim(block, 0, width, axis=dim), axis, backward)
        block = jnp.concatenate([low, block, high], axis=dim)
    return block


def matmul(left_op, right_op):
    return lax.dot_general(
        left_op,
        right_op,
        (((1,), (0,)), ((), ())),
        precision=lax.Precision.HIGHEST,
        preferred_element_type=jnp.float32,
    )


def matmul_tn(left_op, right_op):
    return lax.dot_general(
        left_op,
        right_op,
        (((0,), (0,)), ((), ())),
        precision=lax.Precision.HIGHEST,
        preferred_element_type=jnp.float32,
    )


def matmul_nt(left_op, right_op):
    return lax.dot_general(
        left_op,
        right_op,
        (((1,), (1,)), ((), ())),
        precision=lax.Precision.HIGHEST,
        preferred_element_type=jnp.float32,
    )


def wave_tables(positions):
    freq_index = jnp.arange(K, dtype=jnp.int32) - K // 2
    phase_index = freq_index[:, None] * positions[None, :] % M
    angles = 2.0 * math.pi / M * phase_index.astype(jnp.float32)
    return (jnp.cos(angles), jnp.sin(angles))


def shards(mask_windows, target_windows, pupil_bands, pupil_phase, source_weight):
    src_count = lax.axis_size("src")
    tile_count = lax.axis_size("tile")
    row_count = lax.axis_size("row")
    local_x = mask_windows.shape[1]
    per_device = pupil_phase.shape[0]
    sources = per_device * src_count
    field_scale = 1.0 / (M * K)
    src_id = lax.axis_index("src")
    row_id = lax.axis_index("row")
    x_start = (src_id * row_count + row_id) * local_x
    block_starts = (jnp.arange(src_count, dtype=jnp.int32) * row_count + row_id) * local_x
    row_set = (block_starts[:, None] + jnp.arange(local_x, dtype=jnp.int32)[None, :]).reshape(
        src_count * local_x
    )
    cos_all, sin_all = wave_tables(jnp.arange(M, dtype=jnp.int32))
    cos_set, sin_set = wave_tables(row_set)
    cos_own, sin_own = wave_tables(x_start + jnp.arange(local_x, dtype=jnp.int32))
    window = mask_windows[0]
    goal_block = target_windows[0]
    zero_spec = jnp.zeros((K, K), jnp.float32)
    shard_rows = lax.all_gather(window, ("src", "row"), axis=0, tiled=True)
    part_real = matmul_nt(shard_rows, cos_all)
    part_imag = -matmul_nt(shard_rows, sin_all)
    spec_real = matmul(cos_all, part_real) + matmul(sin_all, part_imag)
    spec_imag = matmul(cos_all, part_imag) - matmul(sin_all, part_real)
    freq_cols = jnp.arange(K, dtype=jnp.int32)
    inside = (freq_cols[None, None, :] >= pupil_bands[:, :, 0:1]) & (
        freq_cols[None, None, :] < pupil_bands[:, :, 1:2]
    )
    passing = inside.astype(jnp.float32)
    pupil_real = passing * jnp.cos(pupil_phase)
    pupil_imag = passing * jnp.sin(pupil_phase)
    amp_real = (pupil_real * spec_real - pupil_imag * spec_imag).reshape(per_device * K, K)
    amp_imag = (pupil_imag * spec_real + pupil_real * spec_imag).reshape(per_device * K, K)
    half_real = (matmul(amp_real, cos_all) - matmul(amp_imag, sin_all)).reshape(per_device, K, M)
    half_imag = (matmul(amp_real, sin_all) + matmul(amp_imag, cos_all)).reshape(per_device, K, M)
    weights = source_weight / sources

    def fields(pair_in):
        one_real, one_imag = pair_in
        field_real = field_scale * (matmul_tn(cos_set, one_real) - matmul_tn(sin_set, one_imag))
        field_imag = field_scale * (matmul_tn(cos_set, one_imag) + matmul_tn(sin_set, one_real))
        return (field_real, field_imag)

    stack_real, stack_imag = lax.map(fields, (half_real, half_imag))
    part_real = stack_real
    part_imag = stack_imag
    intensity = lax.psum_scatter(
        jnp.sum(weights[:, None, None] * (part_real * part_real + part_imag * part_imag), axis=0),
        "src",
        scatter_dimension=0,
        tiled=True,
    )
    resist = jax.nn.sigmoid(STEEPNESS * (intensity - THRESHOLD))
    cotangent = LOSS_SCALE * (resist - goal_block) * STEEPNESS * resist * (1.0 - resist)
    cotangent_all = lax.all_gather(cotangent, "src", axis=0, tiled=True)
    source_ids = jnp.arange(per_device, dtype=jnp.int32)

    def add_back(source_id, totals):
        grad_real, grad_imag, source_terms = totals
        field_real = stack_real[source_id]
        field_imag = stack_imag[source_id]
        back_scale = 2.0 * weights[source_id] * cotangent_all
        back_real = back_scale * field_real
        back_imag = back_scale * field_imag
        adj_real = matmul(cos_set, back_real) + matmul(sin_set, back_imag)
        adj_imag = matmul(cos_set, back_imag) - matmul(sin_set, back_real)
        amp_grad_real = field_scale * (matmul_nt(adj_real, cos_all) + matmul_nt(adj_imag, sin_all))
        amp_grad_imag = field_scale * (matmul_nt(adj_imag, cos_all) - matmul_nt(adj_real, sin_all))
        pass_real = pupil_real[source_id]
        pass_imag = pupil_imag[source_id]
        grad_real = grad_real + pass_real * amp_grad_real + pass_imag * amp_grad_imag
        grad_imag = grad_imag + pass_real * amp_grad_imag - pass_imag * amp_grad_real
        term_value = jnp.sum(cotangent_all * (field_real * field_real + field_imag * field_imag))
        source_terms = source_terms + jnp.where(source_ids == source_id, term_value, 0.0)
        return (grad_real, grad_imag, source_terms)

    grad_real, grad_imag, source_terms = lax.fori_loop(
        0, per_device, add_back, (zero_spec, zero_spec, jnp.zeros((per_device,), jnp.float32))
    )
    grad_real, grad_imag = lax.psum((grad_real, grad_imag), ("src", "row"))
    source_sum = lax.psum(source_terms, ("tile", "row"))
    source_grad = source_sum / (sources * M * tile_count)
    q_one = matmul(grad_real, cos_all) - matmul(grad_imag, sin_all)
    q_two = matmul(grad_real, sin_all) + matmul(grad_imag, cos_all)
    grad_block = matmul_tn(cos_own, q_one) - matmul_tn(sin_own, q_two)
    padded = with_halo(grad_block, (("tile", 1),), OV)
    from_below = padded[:, :OV]
    from_above = padded[:, M + OV :]
    middle = jnp.zeros((local_x, M - 2 * OV), jnp.float32)
    grad_block = grad_block + jnp.concatenate([from_below, middle, from_above], axis=1)
    return (grad_block[None], source_grad)


def solution(mesh):
    return jax.shard_map(
        shards,
        mesh=mesh,
        in_specs=(
            P(("parts", "tile"), ("src", "row"), None),
            P(("parts", "tile"), ("src", "row"), None),
            P(("parts", "src"), None, None),
            P(("parts", "src"), None, None),
            P(("parts", "src")),
        ),
        out_specs=(P(("parts", "tile"), ("src", "row"), None), P(("parts", "src"))),
        check_vma=False,
    )
```

profile of v0, /device:TPU:0, one launch (start us, length us, event | category | flops | bytes accessed | tf_op | source)
XLA Modules:
  0.0 179.0 jit_solution(342020758289789825)
XLA Ops:
  7.2 16.1 %all-gather = f32[1,256,256]{2,1,0:T(8,128)S(1)} all-gather(f32[1,32,256]{2,1,0:T(8,128)} %param.9), channel_id=2, replica_groups=mesh['parts'=2,'src'=4,'tile'=2,'row'=2] {'src','row'}, dimensions={1}, use_global_device_ids=true | all-gather | bytes 294912 | tf_op jit(solution)/shard_map/all_gather | solution.py:86
  23.3 0.9 fusion.123
  24.2 0.9 convolution_negate_fusion
  25.1 0.8 fusion.146
  25.9 0.8 fusion.144
  26.7 0.8 convolution_add_fusion.5
  27.6 0.8 convolution_subtract_fusion.5
  28.5 0.7 multiply_add_fusion
  29.3 1.0 fusion.152
  30.3 1.0 fusion.142
  31.3 1.0 convolution_add_fusion.3
  32.4 1.0 convolution_subtract_fusion.3
  33.6 7.2 %while.35 = (s32[]{:T(128)}, f32[3,128,256]{1,2,0:T(8,128)S(1)}, f32[3,128,256]{1,2,0:T(8,128)S(1)}, f32[3,128,256]{2,1,0:T(8,128)S(1)}, f32[3,128,256]{2,1,0:T(...) while((s32[]{:T(128)}, f32[3,128,256]{1,2,0:T(8,128)S(1)}, ...), condition=%wide.region_1.2_spmd.clone.clone, body=%wide.region_0.1_spmd.clone.clone.sunk | while | flops 202375168 | bytes 1316957 | solution.py:110
  34.2 0.6 fusion.290
  35.4 0.6 fusion.292
  36.6 0.6 fusion.290
  37.8 0.6 fusion.292
  39.0 0.6 fusion.290
  40.9 0.7 copy.22
  41.9 20.5 %reduce-scatter.4.cloned.1.call-done = f32[32,256]{1,0:T(8,128)} async-done(((f32[128,256]{1,0:T(8,128)}), f32[32,256]{1,0:T(8,128)}) %reduce-scatter.4.cloned.1.call-update) | async-done | bytes 32784 | tf_op jit(solution)/shard_map/reduce_scatter | solution.py:113
  62.3 0.8 fusion.163
  63.1 13.5 %all_gather.7 = f32[128,256]{1,0:T(8,128)S(1)} all-gather(f32[32,256]{1,0:T(8,128)S(1)} %fusion.163), channel_id=1, replica_groups=mesh['parts'=2,'src'=4,'tile'=2,'row'=2] {'src'}, dimensions={0}, use_global_device_ids=true | all-gather | bytes 163840 | tf_op jit(solution)/shard_map/all_gather | solution.py:121
  76.7 26.2 %while.36 = (s32[]{:T(128)}, f32[128,128]{1,0:T(8,128)S(1)}, f32[128,128]{1,0:T(8,128)S(1)}, f32[3]{0:T(128)S(1)}, f32[3,128,128]{2,1,0:T(8,128)S(1)}, /*index=5...) while((s32[]{:T(128)}, f32[128,128]{1,0:T(8,128)S(1)}, ...), condition=%wide.region_6.7_spmd.clone.clone.clone.clone, body=%wide.region_4.6_spmd.clone.clone.clone.clone.sunk | while | flops 406126592 | bytes 4593900 | solution.py:143
  78.0 0.6 fusion.306
  78.8 0.6 convolution_add_fusion.7
  79.4 0.6 fusion.304
  80.0 0.6 convolution_subtract_fusion.8
  80.6 0.8 fusion.305
  81.5 0.8 fusion.307
  82.3 0.8 fusion.308
  83.2 0.9 fusion.309
  84.1 0.6 fusion.310
  84.7 0.7 fusion.311
  86.8 0.6 fusion.306
  87.5 0.6 convolution_add_fusion.7
  88.1 0.6 fusion.304
  88.7 0.6 convolution_subtract_fusion.8
  89.4 0.8 fusion.305
  90.2 0.8 fusion.307
  91.1 0.8 fusion.308
  91.9 0.9 fusion.309
  92.8 0.6 fusion.310
  93.4 0.7 fusion.311
  95.5 0.6 fusion.306
  96.2 0.6 convolution_add_fusion.7
  96.8 0.6 fusion.304
  97.5 0.6 convolution_subtract_fusion.8
  98.1 0.8 fusion.305
  98.9 0.9 fusion.307
  99.8 0.8 fusion.308
  100.7 0.9 fusion.309
  101.5 0.6 fusion.310
  102.2 0.7 fusion.311
  102.9 0.6 copy-done.1
  103.5 5.7 %psum.23 = f32[3]{0:T(128)S(1)} all-reduce(f32[3]{0:T(128)S(1)} %get-tuple-element.296), channel_id=1, replica_groups=mesh['parts'=2,'src'=4,'tile'=2,'row'=2] {'tile','row'}, use_global_device_ids=true, to_apply=%region_9.10 | all-reduce | flops 3 | bytes 24 | tf_op jit(solution)/shard_map/psum | solution.py:147
  109.2 47.8 %all-reduce.3.cloned.1.call-done = (f32[128,128]{1,0:T(8,128)}, f32[128,128]{1,0:T(8,128)}) async-done(((f32[128,128]{1,0:T(8,128)}, f32[128,128]{1,0:T(8,128)}), (f32[128,128]{1,0:T(8,128)}, f32[128,128]{1,0:T(8,128)})) %all-reduce.3.cloned.1.call-update) | async-done | bytes 131088 | tf_op jit(solution)/shard_map/psum | solution.py:146
  157.1 1.7 fusion.150
  158.8 0.8 fusion.138
  159.6 0.8 convolution_add_fusion.4
  160.5 0.8 convolution_subtract_fusion.4
  162.5 3.4 %collective-permute-start = (f32[32,32]{1,0:T(8,128)S(1)}, f32[32,32]{1,0:T(8,128)S(1)}, u32[]{:S(2)}, u32[]{:S(2)}) collective-permute-start(f32[32,32]{1,0:T(8,128)S(1)} %get-tuple-element.617), channel_id=1, source_target_pairs={{0,2},{1,3},{4,6},{5,7},{8,10},{9,11},{12,14},{13,15},{16,18},{17,... | collective-permute-start | bytes 12296 | tf_op jit(solution)/shard_map/ppermute | solution.py:20
  165.9 1.3 collective-permute-start.1
  167.7 3.8 %collective-permute-done.1 = f32[32,32]{1,0:T(8,128)S(1)} collective-permute-done((f32[32,32]{1,0:T(8,128)S(1)}, f32[32,32]{1,0:T(8,128)S(1)}, u32[]{:S(2)}, u32[]{:S(2)}) %collective-permute-start.1) | collective-permute-done | bytes 4128 | tf_op jit(solution)/shard_map/ppermute | solution.py:23
  171.5 0.7 fusion.160
  (60 shorter events, 8.9 us)
Async XLA Ops:
  7.2 55.2 %reduce-scatter.4.cloned.1.call-start = ((), (), s32[]{:S(2)}) async-start(), calls=%async_computation.1 | async-start | bytes 163840 | tf_op jit(solution)/shard_map/reduce_scatter | solution.py:113
  27.5 0.8 copy-start.4
  27.6 0.9 copy-start
  33.6 7.2 %copy-start.7 = (f32[3]{0:T(128)S(1)}, f32[3]{0:T(128)}, u32[]{:S(2)}) copy-start(f32[3]{0:T(128)} %param.13) | copy-start | bytes 40
  41.7 20.7 %copy-start.3 = (f32[1,32,256]{2,1,0:T(8,128)S(1)}, f32[1,32,256]{2,1,0:T(8,128)}, u32[]{:S(2)}) copy-start(f32[1,32,256]{2,1,0:T(8,128)} %param.10) | copy-start | bytes 98308
  41.7 115.4 %all-reduce.3.cloned.1.call-start = ((), (), s32[]{:S(2)}) async-start(), calls=%async_computation.2 | async-start | bytes 262144 | tf_op jit(solution)/shard_map/psum | solution.py:146
  102.8 0.6 copy-start.1
  102.9 0.6 copy-start.2
  157.1 1.7 copy-start.6
  158.8 0.8 copy-start.5
  162.5 5.2 %collective-permute-start = (f32[32,32]{1,0:T(8,128)S(1)}, f32[32,32]{1,0:T(8,128)S(1)}, u32[]{:S(2)}, u32[]{:S(2)}) collective-permute-start(f32[32,32]{1,0:T(8,128)S(1)} %get-tuple-element.617), channel_id=1, source_target_pairs={{0,2},{1,3},{4,6},{5,7},{8,10},{9,11},{12,14},{13,15},{16,18},{17,... | collective-permute-start | bytes 12296 | tf_op jit(solution)/shard_map/ppermute | solution.py:20
  165.9 5.6 %collective-permute-start.1 = (f32[32,32]{1,0:T(8,128)S(1)}, f32[32,32]{1,0:T(8,128)S(1)}, u32[]{:S(2)}, u32[]{:S(2)}) collective-permute-start(f32[32,32]{1,0:T(8,128)S(1)} %get-tuple-element.618), channel_id=1, source_target_pairs={{2,0},{3,1},{6,4},{7,5},{10,8},{11,9},{14,12},{15,13},{18,16},{19,... | collective-permute-start | bytes 12296 | tf_op jit(solution)/shard_map/ppermute | solution.py:23
Sparse Core Ops, SparseCore 0:
  41.8 20.4 reduce-scatter.3
  103.6 53.3 all-reduce.2
where the time goes:
time: 179 us
  waiting for transfers between devices  72.2 us (40%)
  matrix products  39.2 us (22%)
  blocking collectives  35.3 us (20%)
  between operations  14.4 us (8%)
  other arithmetic  6.82 us (4%)
  starting transfers between devices  4.74 us (3%)
  local copies, waits for them, and re-layouts  4.13 us (2%)
  loops' own time  2.33 us (1%)
    psum x1, waiting for transfers between devices, shards(): grad_real, grad_imag = lax.psum((grad_real, grad_imag), ('src', 'row'))  47.8 us
    reduce_scatter x1, waiting for transfers between devices, shards(): lax.psum_scatter(jnp.sum(weights[:, None, None] * (part_real * part_real...  20.5 us
    dot_general x24, matrix products, matmul(): lax.dot_general(left_op, right_op, (((1,), (0,)), ((), ())), precision=la...  18.9 us
    all_gather x1, blocking collectives, shards(): shard_rows = lax.all_gather(window, ('src', 'row'), axis=0, tiled=True)  16.1 us
    all_gather x1, blocking collectives, shards(): cotangent_all = lax.all_gather(cotangent, 'src', axis=0, tiled=True)  13.5 us
    dot_general x14, matrix products, matmul_nt(): lax.dot_general(left_op, right_op, (((1,), (1,)), ((), ())), precision=la...  12 us
    dot_general x14, matrix products, matmul_tn(): lax.dot_general(left_op, right_op, (((0,), (0,)), ((), ())), precision=la...  8.24 us
    psum x1, blocking collectives, shards(): source_sum = lax.psum(source_terms, ('tile', 'row'))  5.67 us
  transfers between devices with their start and end apart: 4, of which 3 were waited for; matrix products, arithmetic and copies ran while one was open for 0% of the time, Pallas kernels for 0%

commit v1 on v0

--- a/solution.py
+++ b/solution.py
@@ -10,6 +10,27 @@
 STEEPNESS = 20.0
 THRESHOLD = 0.15
 LOSS_SCALE = 32.0
+
+
+def gather_around(x, axis, dim):
+    size, index, extent = (lax.axis_size(axis), lax.axis_index(axis), x.shape[dim])
+    right = [(i, (i + 1) % size) for i in range(size)]
+    left = [(i, (i - 1) % size) for i in range(size)]
+    out = jnp.zeros((*x.shape[:dim], size * extent, *x.shape[dim + 1 :]), x.dtype)
+    out = lax.dynamic_update_slice_in_dim(out, x, index * extent, axis=dim)
+    from_left = from_right = x
+    half = size // 2
+    for turn in range(1, half + 1):
+        from_left = lax.ppermute(from_left, axis, right)
+        out = lax.dynamic_update_slice_in_dim(
+            out, from_left, (index - turn) % size * extent, axis=dim
+        )
+        if turn < size - half:
+            from_right = lax.ppermute(from_right, axis, left)
+            out = lax.dynamic_update_slice_in_dim(
+                out, from_right, (index + turn) % size * extent, axis=dim
+            )
+    return out
 
 
 def with_halo(block, sides, width):
@@ -118,7 +139,7 @@
     )
     resist = jax.nn.sigmoid(STEEPNESS * (intensity - THRESHOLD))
     cotangent = LOSS_SCALE * (resist - goal_block) * STEEPNESS * resist * (1.0 - resist)
-    cotangent_all = lax.all_gather(cotangent, "src", axis=0, tiled=True)
+    cotangent_all = gather_around(cotangent, "src", 0)
     source_ids = jnp.arange(per_device, dtype=jnp.int32)
 
     def add_back(source_id, totals):

time: 179 us -> 177 us (0.989)
  blocking collectives: 35.3 us -> 21.8 us
  waiting for transfers between devices: 72.2 us -> 79.7 us
  starting transfers between devices: 4.74 us -> 8.68 us
    all_gather x1 -> x0, blocking collectives: 13.5 us -> none  [shards(): cotangent_all = lax.all_gather(cotangent, 'src', axis=0, tiled=True)]
    ppermute x0 -> x3, waiting for transfers between devices: none -> 7.48 us  [the longest x2 7.48 us: gather_around(): from_left = lax.ppermute(from_left, axis, right)]
    ppermute x0 -> x3, starting transfers between devices: none -> 3.94 us  [the longest x1 3.7 us: gather_around(): from_right = lax.ppermute(from_right, axis, left)]
  transfers between devices with their start and end apart: 4 -> 7, of which waited for: 3 -> 5; matrix products, arithmetic and copies ran while one was open for 0% -> 0% of each run, Pallas kernels for 0% -> 0%
where the time goes in v1:
time: 177 us
  waiting for transfers between devices  79.7 us (45%)
  matrix products  39.2 us (22%)
  blocking collectives  21.8 us (12%)
  between operations  14.5 us (8%)
  starting transfers between devices  8.68 us (5%)
  other arithmetic  6.07 us (3%)
  local copies, waits for them, and re-layouts  4.89 us (3%)
  loops' own time  2.33 us (1%)
    psum x1, waiting for transfers between devices, shards(): grad_real, grad_imag = lax.psum((grad_real, grad_imag), ('src', 'row'))  47.7 us
    reduce_scatter x1, waiting for transfers between devices, shards(): lax.psum_scatter(jnp.sum(weights[:, None, None] * (part_real * part_real...  20.6 us
    dot_general x24, matrix products, matmul(): lax.dot_general(left_op, right_op, (((1,), (0,)), ((), ())), precision=la...  18.9 us
    all_gather x1, blocking collectives, shards(): shard_rows = lax.all_gather(window, ('src', 'row'), axis=0, tiled=True)  16.1 us
    dot_general x14, matrix products, matmul_nt(): lax.dot_general(left_op, right_op, (((1,), (1,)), ((), ())), precision=la...  12 us
    dot_general x14, matrix products, matmul_tn(): lax.dot_general(left_op, right_op, (((0,), (0,)), ((), ())), precision=la...  8.28 us
    ppermute x2, waiting for transfers between devices, gather_around(): from_left = lax.ppermute(from_left, axis, right)  7.48 us
    psum x1, blocking collectives, shards(): source_sum = lax.psum(source_terms, ('tile', 'row'))  5.67 us
  transfers between devices with their start and end apart: 7, of which 5 were waited for; matrix products, arithmetic and copies ran while one was open for 0% of the time, Pallas kernels for 0%

profile of v1, /device:TPU:0, one launch (start us, length us, event | category | flops | bytes accessed | tf_op | source)
XLA Modules:
  0.0 177.1 jit_solution(13635740893742940535)
XLA Ops:
  7.2 16.1 %all-gather = f32[1,256,256]{2,1,0:T(8,128)S(1)} all-gather(f32[1,32,256]{2,1,0:T(8,128)} %param.9), channel_id=2, replica_groups=mesh['parts'=2,'src'=4,'tile'=2,'row'=2] {'src','row'}, dimensions={1}, use_global_device_ids=true | all-gather | bytes 294912 | tf_op jit(solution)/shard_map/all_gather | solution.py:107
  23.3 0.9 fusion.123
  24.2 0.9 convolution_negate_fusion
  25.1 0.8 fusion.146
  25.9 0.8 fusion.144
  26.7 0.8 convolution_add_fusion.5
  27.6 0.8 convolution_subtract_fusion.5
  28.5 0.7 multiply_add_fusion
  29.3 1.0 fusion.152
  30.3 1.0 fusion.142
  31.3 1.0 convolution_add_fusion.3
  32.4 1.0 convolution_subtract_fusion.3
  33.6 7.3 %while.35 = (s32[]{:T(128)}, f32[3,128,256]{1,2,0:T(8,128)S(1)}, f32[3,128,256]{1,2,0:T(8,128)S(1)}, f32[3,128,256]{2,1,0:T(8,128)S(1)}, f32[3,128,256]{2,1,0:T(...) while((s32[]{:T(128)}, f32[3,128,256]{1,2,0:T(8,128)S(1)}, ...), condition=%wide.region_1.2_spmd.clone.clone, body=%wide.region_0.1_spmd.clone.clone.sunk | while | flops 202375168 | bytes 1316957 | solution.py:131
  35.4 0.6 fusion.293
  37.8 0.6 fusion.293
  39.0 0.6 fusion.291
  41.0 0.8 copy.28
  41.8 20.6 %reduce-scatter.4.cloned.1.call-done = f32[32,256]{1,0:T(8,128)} async-done(((f32[128,256]{1,0:T(8,128)}), f32[32,256]{1,0:T(8,128)}) %reduce-scatter.4.cloned.1.call-update) | async-done | bytes 32784 | tf_op jit(solution)/shard_map/reduce_scatter | solution.py:134
  62.4 0.7 copy-done.4
  63.6 3.7 %collective-permute-start.1 = (f32[32,256]{1,0:T(8,128)S(1)}, f32[32,256]{1,0:T(8,128)S(1)}, u32[]{:S(2)}, u32[]{:S(2)}) collective-permute-start(f32[32,256]{1,0:T(8,128)S(1)} %get-tuple-element.611), channel_id=1, source_target_pairs={{0,12},{4,0},{8,4},{12,8},{1,13},{5,1},{9,5},{13,9},{2,14},{6,2},{... | collective-permute-start | bytes 98312 | tf_op jit(solution)/shard_map/ppermute | solution.py:29
  67.3 1.8 %collective-permute-done = f32[32,256]{1,0:T(8,128)S(1)} collective-permute-done((f32[32,256]{1,0:T(8,128)S(1)}, f32[32,256]{1,0:T(8,128)S(1)}, u32[]{:S(2)}, u32[]{:S(2)}) %collective-permute-start) | collective-permute-done | bytes 32800 | tf_op jit(solution)/shard_map/ppermute | solution.py:24
  69.2 5.7 %collective-permute-done.2 = f32[32,256]{1,0:T(8,128)S(1)} collective-permute-done((f32[32,256]{1,0:T(8,128)S(1)}, f32[32,256]{1,0:T(8,128)S(1)}, u32[]{:S(2)}, u32[]{:S(2)}) %collective-permute-start.2) | collective-permute-done | bytes 32800 | tf_op jit(solution)/shard_map/ppermute | solution.py:24
  74.8 26.2 %while.36 = (s32[]{:T(128)}, f32[128,128]{1,0:T(8,128)S(1)}, f32[128,128]{1,0:T(8,128)S(1)}, f32[3]{0:T(128)S(1)}, f32[3,128,128]{2,1,0:T(8,128)S(1)}, /*index=5...) while((s32[]{:T(128)}, f32[128,128]{1,0:T(8,128)S(1)}, ...), condition=%wide.region_6.7_spmd.clone.clone.clone.clone, body=%wide.region_4.6_spmd.clone.clone.clone.clone.sunk | while | flops 406126592 | bytes 4593900 | solution.py:164
  76.2 0.6 fusion.307
  76.9 0.6 convolution_add_fusion.7
  77.6 0.6 fusion.305
  78.2 0.6 convolution_subtract_fusion.8
  78.8 0.8 fusion.306
  79.7 0.8 fusion.308
  80.5 0.8 fusion.309
  81.4 0.9 fusion.310
  82.2 0.6 fusion.311
  82.9 0.7 fusion.312
  84.9 0.6 fusion.307
  85.7 0.6 convolution_add_fusion.7
  86.3 0.6 fusion.305
  86.9 0.6 convolution_subtract_fusion.8
  87.5 0.8 fusion.306
  88.4 0.9 fusion.308
  89.2 0.8 fusion.309
  90.1 0.9 fusion.310
  91.0 0.6 fusion.311
  91.6 0.7 fusion.312
  93.7 0.6 fusion.307
  94.4 0.6 convolution_add_fusion.7
  95.0 0.6 fusion.305
  95.6 0.6 convolution_subtract_fusion.8
  96.3 0.8 fusion.306
  97.1 0.8 fusion.308
  98.0 0.8 fusion.309
  98.8 0.9 fusion.310
  99.7 0.6 fusion.311
  100.3 0.7 fusion.312
  101.0 0.6 copy-done.1
  101.7 5.7 %psum.23 = f32[3]{0:T(128)S(1)} all-reduce(f32[3]{0:T(128)S(1)} %get-tuple-element.296), channel_id=1, replica_groups=mesh['parts'=2,'src'=4,'tile'=2,'row'=2] {'tile','row'}, use_global_device_ids=true, to_apply=%region_9.10 | all-reduce | flops 3 | bytes 24 | tf_op jit(solution)/shard_map/psum | solution.py:168
  107.4 47.7 %all-reduce.3.cloned.1.call-done = (f32[128,128]{1,0:T(8,128)}, f32[128,128]{1,0:T(8,128)}) async-done(((f32[128,128]{1,0:T(8,128)}, f32[128,128]{1,0:T(8,128)}), (f32[128,128]{1,0:T(8,128)}, f32[128,128]{1,0:T(8,128)})) %all-reduce.3.cloned.1.call-update) | async-done | bytes 131088 | tf_op jit(solution)/shard_map/psum | solution.py:167
  155.1 1.7 fusion.150
  156.9 0.8 fusion.138
  157.7 0.8 convolution_add_fusion.4
  158.5 0.8 convolution_subtract_fusion.4
  160.5 3.4 %collective-permute-start.3 = (f32[32,32]{1,0:T(8,128)S(1)}, f32[32,32]{1,0:T(8,128)S(1)}, u32[]{:S(2)}, u32[]{:S(2)}) collective-permute-start(f32[32,32]{1,0:T(8,128)S(1)} %get-tuple-element.619), channel_id=1, source_target_pairs={{0,2},{1,3},{4,6},{5,7},{8,10},{9,11},{12,14},{13,15},{16,18},{17,... | collective-permute-start | bytes 12296 | tf_op jit(solution)/shard_map/ppermute | solution.py:41
  163.9 1.3 collective-permute-start.4
  165.7 3.8 %collective-permute-done.4 = f32[32,32]{1,0:T(8,128)S(1)} collective-permute-done((f32[32,32]{1,0:T(8,128)S(1)}, f32[32,32]{1,0:T(8,128)S(1)}, u32[]{:S(2)}, u32[]{:S(2)}) %collective-permute-start.4) | collective-permute-done | bytes 4128 | tf_op jit(solution)/shard_map/ppermute | solution.py:44
  169.5 0.7 fusion.160
  (71 shorter events, 10.4 us)
Async XLA Ops:
  7.2 55.2 %reduce-scatter.4.cloned.1.call-start = ((), (), s32[]{:S(2)}) async-start(), calls=%async_computation.1 | async-start | bytes 163840 | tf_op jit(solution)/shard_map/reduce_scatter | solution.py:134
  27.5 0.8 copy-start.5
  27.6 0.9 copy-start
  33.6 7.3 %copy-start.8 = (f32[3]{0:T(128)S(1)}, f32[3]{0:T(128)}, u32[]{:S(2)}) copy-start(f32[3]{0:T(128)} %param.13) | copy-start | bytes 40
  41.8 113.4 %all-reduce.3.cloned.1.call-start = ((), (), s32[]{:S(2)}) async-start(), calls=%async_computation.2 | async-start | bytes 262144 | tf_op jit(solution)/shard_map/psum | solution.py:167
  41.8 20.6 %copy-start.3 = (f32[1,32,256]{2,1,0:T(8,128)S(1)}, f32[1,32,256]{2,1,0:T(8,128)}, u32[]{:S(2)}) copy-start(f32[1,32,256]{2,1,0:T(8,128)} %param.10) | copy-start | bytes 98308
  62.4 0.8 copy-start.4
  63.2 5.9 %collective-permute-start = (f32[32,256]{1,0:T(8,128)S(1)}, f32[32,256]{1,0:T(8,128)S(1)}, u32[]{:S(2)}, u32[]{:S(2)}) collective-permute-start(f32[32,256]{1,0:T(8,128)S(1)} %get-tuple-element.611), channel_id=1, source_target_pairs={{0,4},{4,8},{8,12},{12,0},{1,5},{5,9},{9,13},{13,1},{2,6},{6,10},{... | collective-permute-start | bytes 98312 | tf_op jit(solution)/shard_map/ppermute | solution.py:24
  63.6 5.5 %collective-permute-start.1 = (f32[32,256]{1,0:T(8,128)S(1)}, f32[32,256]{1,0:T(8,128)S(1)}, u32[]{:S(2)}, u32[]{:S(2)}) collective-permute-start(f32[32,256]{1,0:T(8,128)S(1)} %get-tuple-element.611), channel_id=1, source_target_pairs={{0,12},{4,0},{8,4},{12,8},{1,13},{5,1},{9,5},{13,9},{2,14},{6,2},{... | collective-permute-start | bytes 98312 | tf_op jit(solution)/shard_map/ppermute | solution.py:29
  69.1 5.7 %collective-permute-start.2 = (f32[32,256]{1,0:T(8,128)S(1)}, f32[32,256]{1,0:T(8,128)S(1)}, u32[]{:S(2)}, u32[]{:S(2)}) collective-permute-start(f32[32,256]{1,0:T(8,128)S(1)} %collective-permute-done), channel_id=1, source_target_pairs={{0,4},{4,8},{8,12},{12,0},{1,5},{5,9},{9,13},{13,1},{2,6},{6,10},{... | collective-permute-start | bytes 98312 | tf_op jit(solution)/shard_map/ppermute | solution.py:24
  101.0 0.6 copy-start.1
  101.0 0.6 copy-start.2
  155.1 1.7 copy-start.7
  156.9 0.8 copy-start.6
  160.5 5.2 %collective-permute-start.3 = (f32[32,32]{1,0:T(8,128)S(1)}, f32[32,32]{1,0:T(8,128)S(1)}, u32[]{:S(2)}, u32[]{:S(2)}) collective-permute-start(f32[32,32]{1,0:T(8,128)S(1)} %get-tuple-element.619), channel_id=1, source_target_pairs={{0,2},{1,3},{4,6},{5,7},{8,10},{9,11},{12,14},{13,15},{16,18},{17,... | collective-permute-start | bytes 12296 | tf_op jit(solution)/shard_map/ppermute | solution.py:41
  163.9 5.6 %collective-permute-start.4 = (f32[32,32]{1,0:T(8,128)S(1)}, f32[32,32]{1,0:T(8,128)S(1)}, u32[]{:S(2)}, u32[]{:S(2)}) collective-permute-start(f32[32,32]{1,0:T(8,128)S(1)} %get-tuple-element.620), channel_id=1, source_target_pairs={{2,0},{3,1},{6,4},{7,5},{10,8},{11,9},{14,12},{15,13},{18,16},{19,... | collective-permute-start | bytes 12296 | tf_op jit(solution)/shard_map/ppermute | solution.py:44
Sparse Core Ops, SparseCore 0:
  41.9 20.4 reduce-scatter.3
  101.8 53.2 all-reduce.2
